TPU v7x, 128 devices: a whole 4x4x4 slice. The times are simulated.
128 devices in a mesh: node: 32 (over z, y_lo, x), rep: 4 (over y_hi, core).
Axes of the slice: x: 4, y: 4 (y_hi: 2, y_lo: 2; y = y_hi * 2 + y_lo), z: 4, core: 2. Of those that a mesh axis runs over, the one named last changes fastest.
Arguments:
- node_feats: bfloat16 [65536, 256], P('node'), may hold values from -6 to 6
- weight: bfloat16 [256, 256], replicated, may hold values from -0.375 to 0.375
- cotangent: bfloat16 [65536, 256], P(('node', 'rep')), may hold values from -6 to 6
- tiles: bfloat16 [32, 4, 160, 256, 256], P('node', 'rep'), may hold values from -0.049804688 to 0.049804688
- tile_rows: int32 [32, 4, 160], P('node', 'rep'), may hold values from 0 to 7
- tile_cols: int32 [32, 4, 160], P('node', 'rep'), may hold values from 0 to 63
- tile_count: int32 [32, 4], P('node', 'rep'), may hold values from 80 to 160, as said below
Outputs:
- activated: bfloat16 [65536, 256], P(('node', 'rep'))
- feature_grad: bfloat16 [65536, 256], P(('node', 'rep'))
- weight_grad: float32 [256, 256], replicated
Inputs may be any that keep to these rules, and one draw needn't show every extreme that they name: `tile_count`: slots at and beyond a device's count are ignored; some device has all 160 slots live in every draw.
All inputs are finite; a program needn't handle non-finite values.
Results may differ from a plain program's by a relative error of at most 0.007.
Values may be sent and summed in bfloat16 or wider, within the bound.
No kernel may reach another device: no remote copies, remote signals or barrier semaphores. Data moves between devices by JAX's collectives and lax.ppermute only.
A program may use at most 256 MiB of HBM per device.

v0:
```python
import jax
import jax.numpy as jnp
from jax import lax
from jax.sharding import PartitionSpec as P


def body(node_feats, weight, cotangent, tiles, tile_rows, tile_cols, tile_count):
    nrep = lax.axis_size("rep")
    nnode = lax.axis_size("node")
    rep_idx = lax.axis_index("rep")
    rows, feat = node_feats.shape
    block = tiles.shape[-1]
    row_blocks = rows // block
    quarter = row_blocks // nrep
    share = rows // nrep
    compact_cols = quarter * nnode
    slot_tiles = tiles[0, 0]
    slot_rows = tile_rows[0, 0]
    slot_cols = tile_cols[0, 0]
    slot_total = slot_tiles.shape[0]
    live = jnp.arange(slot_total, dtype=jnp.int32) < tile_count[0, 0]
    live_scale = live.astype(jnp.float32)[:, None, None]
    feat_blocks = node_feats.reshape(row_blocks, block, feat)
    mine = lax.dynamic_slice_in_dim(feat_blocks, rep_idx * quarter, quarter, 0)
    compact = lax.all_gather(mine, "node", axis=0, tiled=True)
    picked = compact[slot_cols]
    forward_prod = (
        jnp.einsum("tab,tbf->taf", slot_tiles, picked, preferred_element_type=jnp.float32)
        * live_scale
    )
    partial_agg = (
        jnp.zeros((row_blocks, block, feat), jnp.float32)
        .at[slot_rows]
        .add(forward_prod)
        .reshape(rows, feat)
    )
    scale = float(rows * nnode) ** (-0.5)
    aggregated = lax.psum(partial_agg, "rep").astype(jnp.bfloat16)
    cot_full = lax.all_gather(cotangent, "rep", axis=0, tiled=True)
    pre = jnp.dot(aggregated, weight, preferred_element_type=jnp.float32)
    sig = jax.nn.sigmoid(pre)
    activated_full = (pre * sig).astype(jnp.bfloat16)
    dpre = (cot_full.astype(jnp.float32) * sig * (1.0 + pre * (1.0 - sig))).astype(jnp.bfloat16)
    dagg = jnp.dot(dpre, weight.T, preferred_element_type=jnp.float32).astype(jnp.bfloat16)
    activated = lax.dynamic_slice_in_dim(activated_full, rep_idx * share, share, 0)
    agg_share = lax.dynamic_slice_in_dim(aggregated, rep_idx * share, share, 0)
    dpre_share = lax.dynamic_slice_in_dim(dpre, rep_idx * share, share, 0)
    weight_term = lax.dot_general(
        agg_share, dpre_share, (((0,), (0,)), ((), ())), preferred_element_type=jnp.float32
    )
    weight_grad = lax.psum(weight_term, ("node", "rep")) * scale
    dagg_blocks = dagg.reshape(row_blocks, block, feat)
    backward_prod = (
        jnp.einsum(
            "tab,taf->tbf", slot_tiles, dagg_blocks[slot_rows], preferred_element_type=jnp.float32
        )
        * live_scale
    )
    column_part = (
        jnp.zeros((compact_cols, block, feat), jnp.float32).at[slot_cols].add(backward_prod)
    )
    owned = lax.psum_scatter(column_part, "node", scatter_dimension=0, tiled=True)
    feature_grad = owned.reshape(quarter * block, feat).astype(jnp.bfloat16)
    return (activated, feature_grad, weight_grad)


def solution(mesh):
    placed = (
        P("node", None),
        P(),
        P(("node", "rep"), None),
        P("node", "rep", None, None, None),
        P("node", "rep", None),
        P("node", "rep", None),
        P("node", "rep"),
    )
    return jax.shard_map(
        body,
        mesh=mesh,
        in_specs=placed,
        out_specs=(P(("node", "rep"), None), P(("node", "rep"), None), P()),
        check_vma=False,
    )
```

profile of v0, /device:TPU:0, one launch (start us, length us, event | category | flops | bytes accessed | tf_op | source)
XLA Modules:
  0.0 760.6 jit_solution(5284792371590088112)
XLA Ops:
  7.2 1.2 copy-done
  8.4 0.7 constant_dynamic-slice_fusion
  9.2 0.7 all-gather.5.cloned.1.call-update
  9.9 0.7 compare_select_fusion
  11.3 0.7 compare_select_fusion.1
  12.0 167.9 %all-gather.3.cloned.1.call-done = bf16[64,256,256]{2,1,0:T(8,128)(2,1)} async-done(((bf16[2,256,256]{2,1,0:T(8,128)(2,1)}), bf16[64,256,256]{2,1,0:T(8,128)(2,1)}) %all-gather.3.cloned.1.call-update) | async-done | bytes 8388624 | tf_op jit(solution)/shard_map/all_gather | solution.py:25
  179.9 13.0 %gather_fusion = bf16[160,256,256]{2,1,0:T(8,128)(2,1)} fusion(bf16[64,256,256]{2,1,0:T(8,128)(2,1)} %all-gather.3.cloned.1.call-done, s32[1024]{0:T(1024)S(1)} %pad_clamp_fusion.1), kind=kCustom, calls=%fused_computation | custom fusion | bytes 41943680 | tf_op jit(solution)/shard_map/gather | solution.py:26
  192.9 30.3 %multiply_bitcast_fusion.1 = f32[160,256,256]{1,2,0:T(8,128)} fusion(f32[160]{0:T(256)S(1)} %compare_convert_fusion, bf16[160,256,256]{2,1,0:T(8,128)(2,1)} %gather_fusion, bf16[1,1,160,256,256]{4,3,2,1,0:T(8,128)(2,1)} %param.10), kind=kOutput, calls=%fused_computation.5 | convolution fusion | flops 5379194880 | bytes 83886720 | tf_op jit(solution)/shard_map/tab,tbf->taf/dot_general | solution.py:28
  223.2 41.6 %copy.17 = f32[160,256,256]{2,1,0:T(8,128)} copy(f32[160,256,256]{1,2,0:T(8,128)} %multiply_bitcast_fusion.1) | data formatting | bytes 83886080 | tf_op jit(solution)/shard_map/mul | solution.py:28
  265.0 56.7 %scatter_fusion = f32[8,256,256]{2,1,0:T(8,128)S(1)} fusion(f32[8,256,256]{2,1,0:T(8,128)S(1)} %broadcast_in_dim.4, s32[160]{0:T(256)S(1)} %bitcast.38, f32[160,256,256]{2,1,0:T(8,128)} %copy.17), kind=kCustom, calls=%fused_computation.2 | custom fusion | flops 10485760 | bytes 125829760 | tf_op jit(solution)/shard_map/scatter-add | solution.py:34
  321.7 42.3 %all-reduce.4 = bf16[2048,256]{1,0:T(8,128)(2,1)S(1)} all-reduce(f32[2048,256]{1,0:T(8,128)S(1)} %bitcast.32), channel_id=1, replica_groups=mesh['node'=32,'rep'=4] {'rep'}, use_global_device_ids=true, to_apply=%region_1.0 | all-reduce | flops 524288 | bytes 3145728 | tf_op jit(solution)/shard_map/psum | solution.py:38
  364.1 3.8 multiply_convert_fusion
  367.8 0.5 convolution_convert_fusion
  368.3 1.9 fusion.9
  370.3 0.2 reduce-scatter.2.cloned.1.call-start
  370.5 9.6 %gather_fusion.1 = bf16[160,256,256]{2,1,0:T(8,128)(2,1)} fusion(bf16[8,256,256]{2,1,0:T(8,128)(2,1)S(1)} %bitcast.33, s32[1024]{0:T(1024)S(1)} %pad_clamp_fusion), kind=kCustom, calls=%fused_computation.1 | custom fusion | bytes 41943680 | tf_op jit(solution)/shard_map/gather | solution.py:55
  380.1 26.6 %multiply_bitcast_fusion = f32[160,256,256]{1,2,0:T(8,128)} fusion(f32[160]{0:T(256)S(1)} %compare_convert_fusion, bf16[160,256,256]{2,1,0:T(8,128)(2,1)} %gather_fusion.1, bf16[1,1,160,256,256]{4,3,2,1,0:T(8,128)(2,1)} %param.10), kind=kOutput, calls=%fused_computation.4 | convolution fusion | flops 5379194880 | bytes 83886720 | tf_op jit(solution)/shard_map/tab,taf->tbf/dot_general | solution.py:54
  406.7 41.7 %copy.19 = f32[160,256,256]{2,1,0:T(8,128)} copy(f32[160,256,256]{1,2,0:T(8,128)} %multiply_bitcast_fusion) | data formatting | bytes 83886080 | tf_op jit(solution)/shard_map/mul | solution.py:54
  448.3 7.8 %broadcast_in_dim.5 = f32[64,256,256]{2,1,0:T(8,128)} broadcast(f32[]{:T(128)} %constant.10.clone.1), dimensions={} | broadcast | bytes 16777220 | tf_op jit(solution)/shard_map/broadcast_in_dim | solution.py:60
  456.1 91.3 %scatter_fusion.1 = f32[64,256,256]{2,1,0:T(8,128)} fusion(f32[64,256,256]{2,1,0:T(8,128)} %broadcast_in_dim.5, s32[160]{0:T(256)S(1)} %bitcast.36, f32[160,256,256]{2,1,0:T(8,128)} %copy.19), kind=kCustom, calls=%fused_computation.3 | custom fusion | flops 10485760 | bytes 125829760 | tf_op jit(solution)/shard_map/scatter-add | solution.py:60
  547.5 1.8 fusion.8
  549.3 1.7 broadcast_multiply_fusion
  550.9 201.3 %reduce-scatter.2.cloned.1.call-done = f32[2,256,256]{2,1,0:T(8,128)} async-done(((f32[64,256,256]{2,1,0:T(8,128)}), f32[2,256,256]{2,1,0:T(8,128)}) %reduce-scatter.2.cloned.1.call-update) | async-done | bytes 524304 | tf_op jit(solution)/shard_map/reduce_scatter | solution.py:62
  752.3 1.8 convert_element_type.34
  (23 shorter events, 0.4 us)
Async XLA Ops:
  7.2 1.2 copy-start
  7.2 172.7 %all-gather.3.cloned.1.call-start = ((), (), s32[]{:S(2)}) async-start(), calls=%async_computation.1 | async-start | bytes 8650752 | tf_op jit(solution)/shard_map/all_gather | solution.py:25
  9.1 354.9 %all-gather.5.cloned.1.call-start = ((), (), s32[]{:S(2)}) async-start(), calls=%async_computation.2 | async-start | bytes 1310720 | tf_op jit(solution)/shard_map/all_gather | solution.py:39
  9.9 539.4 %all-reduce.3.cloned.1.call-start = ((), (), s32[]{:S(2)}) async-start(), calls=%async_computation.4 | async-start | bytes 524288 | tf_op jit(solution)/shard_map/psum | solution.py:51
  10.6 182.3 %copy-start.4 = (s32[160,1]{0,1:T(1,128)}, s32[160,1]{0,1:T(1,128)S(1)}, u32[]{:S(2)}) copy-start(s32[160,1]{0,1:T(1,128)S(1)} %compare_select_fusion) | copy-start | bytes 1924
  265.0 99.0 %copy-start.3 = (bf16[256,256]{1,0:T(8,128)(2,1)S(1)}, bf16[256,256]{1,0:T(8,128)(2,1)}, u32[]{:S(2)}) copy-start(bf16[256,256]{1,0:T(8,128)(2,1)} %param.8) | copy-start | bytes 393220
  364.0 3.8 copy-start.2
  370.3 382.0 %reduce-scatter.2.cloned.1.call-start = ((), (), s32[]{:S(2)}) async-start(), calls=%async_computation.3 | async-start | bytes 17301504 | tf_op jit(solution)/shard_map/reduce_scatter | solution.py:62
  406.7 49.5 %copy-start.5 = (s32[160,1]{0,1:T(1,128)S(1)}, s32[160,1]{0,1:T(1,128)}, u32[]{:S(2)}) copy-start(s32[160,1]{0,1:T(1,128)} %copy-done.4) | copy-start | bytes 1924
  456.1 297.9 %copy-start.1 = (bf16[2048,256]{1,0:T(8,128)(2,1)S(1)}, bf16[2048,256]{1,0:T(8,128)(2,1)}, u32[]{:S(2)}) copy-start(bf16[2048,256]{1,0:T(8,128)(2,1)} %param.7) | copy-start | bytes 3145732
Sparse Core Ops, SparseCore 0:
  10.2 169.6 all-gather.2
  181.6 21.7 all-gather.4
  370.4 142.5 all-reduce.2
  547.6 204.6 reduce-scatter.1
where the time goes:
time: 763 us; the launch traced here: 761 us
  waiting for transfers between devices  370 us (48%)
  other arithmetic  155 us (20%)
  local copies, waits for them, and re-layouts  116 us (15%)
  matrix products  63 us (8%)
  blocking collectives  42.3 us (6%)
  between operations  14.5 us (2%)
    reduce_scatter x1, waiting for transfers between devices, body(): lax.psum_scatter(column_part, 'node', scatter_dimension=0, tiled=True)  201 us
    all_gather x1, waiting for transfers between devices, body(): compact = lax.all_gather(mine, 'node', axis=0, tiled=True)  168 us
    scatter-add x1, other arithmetic, body(): jnp.zeros((compact_cols, block, feat), jnp.float32).at[slot_cols]  91.3 us
    scatter-add x1, other arithmetic, body(): partial_agg = jnp.zeros((row_blocks, block, feat), jnp.float32).at[slot_r...  56.7 us
    psum x1, blocking collectives, body(): aggregated = lax.psum(partial_agg, 'rep').astype(jnp.bfloat16)  42.3 us
    mul x1, local copies, waits for them, and re-layouts, body(): jnp.einsum('tab,taf->tbf', slot_tiles, dagg_blocks[slot_rows], preferred_...  41.7 us
    mul x1, local copies, waits for them, and re-layouts, body(): jnp.einsum('tab,tbf->taf', slot_tiles, picked, preferred_element_type=jnp...  41.6 us
    dot_general x1, matrix products, body(): jnp.einsum('tab,tbf->taf', slot_tiles, picked, preferred_element_type=jnp...  30.3 us
  transfers between devices with their start and end apart: 4, of which 2 were waited for; matrix products, arithmetic and copies ran while one was open for 43% of the time, Pallas kernels for 0%

commit v1 on v0

--- a/solution.py
+++ b/solution.py
@@ -35,7 +35,7 @@
         .reshape(rows, feat)
     )
     scale = float(rows * nnode) ** (-0.5)
-    aggregated = lax.psum(partial_agg, "rep").astype(jnp.bfloat16)
+    aggregated = jnp.sum(lax.all_gather(partial_agg, "rep"), axis=0).astype(jnp.bfloat16)
     cot_full = lax.all_gather(cotangent, "rep", axis=0, tiled=True)
     pre = jnp.dot(aggregated, weight, preferred_element_type=jnp.float32)
     sig = jax.nn.sigmoid(pre)

time: 763 us -> 805 us (1.055)
  waiting for transfers between devices: 370 us -> 449 us
  blocking collectives: 42.3 us -> 0 us
    all_gather x0 -> x1, waiting for transfers between devices: none -> 62.5 us  [body(): lax.all_gather(partial_agg, 'rep')]
    psum x1 -> x0, blocking collectives: 42.3 us -> none  [body(): aggregated = lax.psum(partial_agg, 'rep').astype(jnp.bfloat16)]
    all_gather x1, waiting for transfers between devices: 0.02 us -> 17.6 us  [body(): cot_full = lax.all_gather(cotangent, 'rep', axis=0, tiled=True)]
  transfers between devices with their start and end apart: 4 -> 5, of which waited for: 2 -> 4; matrix products, arithmetic and copies ran while one was open for 43% -> 23% of each run, Pallas kernels for 0% -> 0%
where the time goes in v1:
time: 805 us; the launch traced here: 803 us
  waiting for transfers between devices  449 us (56%)
  other arithmetic  159 us (20%)
  local copies, waits for them, and re-layouts  117 us (15%)
  matrix products  62.4 us (8%)
  between operations  14.5 us (2%)
    reduce_scatter x1, waiting for transfers between devices, body(): lax.psum_scatter(column_part, 'node', scatter_dimension=0, tiled=True)  200 us
    all_gather x1, waiting for transfers between devices, body(): compact = lax.all_gather(mine, 'node', axis=0, tiled=True)  169 us
    scatter-add x1, other arithmetic, body(): jnp.zeros((compact_cols, block, feat), jnp.float32).at[slot_cols]  91.1 us
    all_gather x1, waiting for transfers between devices, body(): lax.all_gather(partial_agg, 'rep')  62.5 us
    scatter-add x1, other arithmetic, body(): partial_agg = jnp.zeros((row_blocks, block, feat), jnp.float32).at[slot_r...  56.7 us
    mul x1, local copies, waits for them, and re-layouts, body(): jnp.einsum('tab,taf->tbf', slot_tiles, dagg_blocks[slot_rows], preferred_...  41.7 us
    mul x1, local copies, waits for them, and re-layouts, body(): jnp.einsum('tab,tbf->taf', slot_tiles, picked, preferred_element_type=jnp...  41.6 us
    dot_general x1, matrix products, body(): jnp.einsum('tab,tbf->taf', slot_tiles, picked, preferred_element_type=jnp...  30.3 us
  transfers between devices with their start and end apart: 5, of which 4 were waited for; matrix products, arithmetic and copies ran while one was open for 23% of the time, Pallas kernels for 0%

profile of v1, /device:TPU:0, one launch (start us, length us, event | category | flops | bytes accessed | tf_op | source)
XLA Modules:
  0.0 802.6 jit_solution(8371043184359536447)
XLA Ops:
  7.2 1.2 copy-done
  8.4 0.7 constant_dynamic-slice_fusion
  9.8 0.7 compare_select_fusion
  10.5 0.7 compare_select_fusion.1
  11.2 168.7 %all-gather.4.cloned.1.call-done = bf16[64,256,256]{2,1,0:T(8,128)(2,1)} async-done(((bf16[2,256,256]{2,1,0:T(8,128)(2,1)}), bf16[64,256,256]{2,1,0:T(8,128)(2,1)}) %all-gather.4.cloned.1.call-update) | async-done | bytes 8388624 | tf_op jit(solution)/shard_map/all_gather | solution.py:25
  179.9 13.0 %gather_fusion = bf16[160,256,256]{2,1,0:T(8,128)(2,1)} fusion(bf16[64,256,256]{2,1,0:T(8,128)(2,1)} %all-gather.4.cloned.1.call-done, s32[1024]{0:T(1024)S(1)} %pad_clamp_fusion.1), kind=kCustom, calls=%fused_computation | custom fusion | bytes 41943680 | tf_op jit(solution)/shard_map/gather | solution.py:26
  192.9 30.3 %multiply_bitcast_fusion.1 = f32[160,256,256]{1,2,0:T(8,128)} fusion(f32[160]{0:T(256)S(1)} %compare_convert_fusion, bf16[160,256,256]{2,1,0:T(8,128)(2,1)} %gather_fusion, bf16[1,1,160,256,256]{4,3,2,1,0:T(8,128)(2,1)} %param.10), kind=kOutput, calls=%fused_computation.5 | convolution fusion | flops 5379194880 | bytes 83886720 | tf_op jit(solution)/shard_map/tab,tbf->taf/dot_general | solution.py:28
  223.2 41.6 %copy.17 = f32[160,256,256]{2,1,0:T(8,128)} copy(f32[160,256,256]{1,2,0:T(8,128)} %multiply_bitcast_fusion.1) | data formatting | bytes 83886080 | tf_op jit(solution)/shard_map/mul | solution.py:28
  265.0 56.7 %scatter_fusion = f32[8,256,256]{2,1,0:T(8,128)S(1)} fusion(f32[8,256,256]{2,1,0:T(8,128)S(1)} %broadcast_in_dim.4, s32[160]{0:T(256)S(1)} %bitcast.37, f32[160,256,256]{2,1,0:T(8,128)} %copy.17), kind=kCustom, calls=%fused_computation.2 | custom fusion | flops 10485760 | bytes 125829760 | tf_op jit(solution)/shard_map/scatter-add | solution.py:34
  321.7 1.3 copy-done.2
  323.9 62.5 %all-gather.6.cloned.1.call-done = f32[4,2048,256]{2,1,0:T(8,128)} async-done(((f32[1,2048,256]{2,1,0:T(8,128)}), f32[4,2048,256]{2,1,0:T(8,128)}) %all-gather.6.cloned.1.call-update) | async-done | bytes 8388624 | tf_op jit(solution)/shard_map/all_gather | solution.py:38
  386.4 4.2 reduce_sum.9
  390.6 17.6 %all-gather.8.cloned.1.call-done = bf16[2048,256]{1,0:T(8,128)(2,1)} async-done(((bf16[512,256]{1,0:T(8,128)(2,1)}), bf16[2048,256]{1,0:T(8,128)(2,1)}) %all-gather.8.cloned.1.call-update) | async-done | bytes 1048592 | tf_op jit(solution)/shard_map/all_gather | solution.py:39
  408.3 4.0 multiply_convert_fusion
  412.8 1.0 fusion.9
  414.0 9.6 %gather_fusion.1 = bf16[160,256,256]{2,1,0:T(8,128)(2,1)} fusion(bf16[8,256,256]{2,1,0:T(8,128)(2,1)S(1)} %bitcast.33, s32[1024]{0:T(1024)S(1)} %pad_clamp_fusion), kind=kCustom, calls=%fused_computation.1 | custom fusion | bytes 41943680 | tf_op jit(solution)/shard_map/gather | solution.py:55
  423.6 26.6 %multiply_bitcast_fusion = f32[160,256,256]{1,2,0:T(8,128)} fusion(f32[160]{0:T(256)S(1)} %compare_convert_fusion, bf16[160,256,256]{2,1,0:T(8,128)(2,1)} %gather_fusion.1, bf16[1,1,160,256,256]{4,3,2,1,0:T(8,128)(2,1)} %param.10), kind=kOutput, calls=%fused_computation.4 | convolution fusion | flops 5379194880 | bytes 83886720 | tf_op jit(solution)/shard_map/tab,taf->tbf/dot_general | solution.py:54
  450.3 41.7 %copy.19 = f32[160,256,256]{2,1,0:T(8,128)} copy(f32[160,256,256]{1,2,0:T(8,128)} %multiply_bitcast_fusion) | data formatting | bytes 83886080 | tf_op jit(solution)/shard_map/mul | solution.py:54
  491.9 7.8 broadcast_in_dim.5
  499.7 91.1 %scatter_fusion.1 = f32[64,256,256]{2,1,0:T(8,128)} fusion(f32[64,256,256]{2,1,0:T(8,128)} %broadcast_in_dim.5, s32[160]{0:T(256)S(1)} %bitcast.36, f32[160,256,256]{2,1,0:T(8,128)} %copy.19), kind=kCustom, calls=%fused_computation.3 | custom fusion | flops 10485760 | bytes 125829760 | tf_op jit(solution)/shard_map/scatter-add | solution.py:60
  590.9 2.0 fusion.8
  592.9 1.7 broadcast_multiply_fusion
  594.5 199.8 %reduce-scatter.2.cloned.1.call-done = f32[2,256,256]{2,1,0:T(8,128)} async-done(((f32[64,256,256]{2,1,0:T(8,128)}), f32[2,256,256]{2,1,0:T(8,128)}) %reduce-scatter.2.cloned.1.call-update) | async-done | bytes 524304 | tf_op jit(solution)/shard_map/reduce_scatter | solution.py:62
  794.3 1.8 convert_element_type.34
  (26 shorter events, 1.8 us)
Async XLA Ops:
  7.2 1.2 copy-start
  7.2 172.7 %all-gather.4.cloned.1.call-start = ((), (), s32[]{:S(2)}) async-start(), calls=%async_computation.1 | async-start | bytes 8650752 | tf_op jit(solution)/shard_map/all_gather | solution.py:25
  9.1 377.2 %all-gather.6.cloned.1.call-start = ((), (), s32[]{:S(2)}) async-start(), calls=%async_computation.2 | async-start | bytes 10485760 | tf_op jit(solution)/shard_map/all_gather | solution.py:38
  10.5 182.3 %copy-start.4 = (s32[160,1]{0,1:T(1,128)}, s32[160,1]{0,1:T(1,128)S(1)}, u32[]{:S(2)}) copy-start(s32[160,1]{0,1:T(1,128)S(1)} %compare_select_fusion) | copy-start | bytes 1924
  265.0 143.3 %copy-start.3 = (bf16[256,256]{1,0:T(8,128)(2,1)S(1)}, bf16[256,256]{1,0:T(8,128)(2,1)}, u32[]{:S(2)}) copy-start(bf16[256,256]{1,0:T(8,128)(2,1)} %param.8) | copy-start | bytes 393220
  321.7 1.4 copy-start.2
  323.1 85.2 %all-gather.8.cloned.1.call-start = ((), (), s32[]{:S(2)}) async-start(), calls=%async_computation.3 | async-start | bytes 1310720 | tf_op jit(solution)/shard_map/all_gather | solution.py:39
  323.8 269.1 %all-reduce.2.cloned.1.call-start = ((), (), s32[]{:S(2)}) async-start(), calls=%async_computation.5 | async-start | bytes 524288 | tf_op jit(solution)/shard_map/psum | solution.py:51
  413.8 380.5 %reduce-scatter.2.cloned.1.call-start = ((), (), s32[]{:S(2)}) async-start(), calls=%async_computation.4 | async-start | bytes 17301504 | tf_op jit(solution)/shard_map/reduce_scatter | solution.py:62
  450.3 49.5 %copy-start.5 = (s32[160,1]{0,1:T(1,128)S(1)}, s32[160,1]{0,1:T(1,128)}, u32[]{:S(2)}) copy-start(s32[160,1]{0,1:T(1,128)} %copy-done.4) | copy-start | bytes 1924
  499.7 296.4 %copy-start.1 = (bf16[2048,256]{1,0:T(8,128)(2,1)S(1)}, bf16[2048,256]{1,0:T(8,128)(2,1)}, u32[]{:S(2)}) copy-start(bf16[2048,256]{1,0:T(8,128)(2,1)} %param.7) | copy-start | bytes 3145732
Sparse Core Ops, SparseCore 0:
  10.2 169.6 all-gather.3
  323.2 63.1 all-gather.5
  388.1 20.1 all-gather.7
  413.9 141.3 all-reduce.1
  591.0 203.2 reduce-scatter.1
